TPU v7x, 512 devices: a whole 4x8x8 slice. The times are simulated.
512 devices in a mesh: samp: 32 (over x, z), blk: 16 (over y, core).
Axes of the slice: x: 4, y: 8, z: 8, core: 2. Of those that a mesh axis runs over, the one named last changes fastest.
Arguments:
- dosages: int32 [49152, 8192], P('samp', 'blk'), may hold values from 0 to 2, as said below
- new_dosages: int32 [49152, 2048], P('samp', 'blk'), may hold values from 0 to 2, as said below
- traits: float32 [64, 49152], P(None, 'samp'), may hold values from -40 to 40
- shrink: float32 [5], replicated, may hold values from 0.5 to 5
Outputs:
- residual: float32 [5, 64, 49152], P(None, 'blk', 'samp')
- scores: float32 [5, 64, 2048], P(None, None, 'blk')
Inputs may be any that keep to these rules, and one draw needn't show every extreme that they name: `dosages`: codes of haplotype pairs, with linkage along neighbouring variants. `new_dosages`: codes of haplotype pairs, with linkage along neighbouring variants.
All inputs are finite; a program needn't handle non-finite values.
Results may differ from a plain program's by a relative error of at most 0.0053.
Values may be sent and summed in bfloat16 or wider, within the bound.
No kernel may reach another device: no remote copies, remote signals or barrier semaphores. Data moves between devices by JAX's collectives and lax.ppermute only.
A program may use at most 64 MiB of HBM per device.

v0:
```python
import jax
import jax.numpy as jnp
from jax import lax
from jax.sharding import PartitionSpec as P

RIDGE = 5
CHEB = 3


def chebyshev(rhs_cols, apply_fn, centre, half_width, sweeps):
    sig_ratio = centre / half_width
    factor = 1.0 / sig_ratio
    direction = rhs_cols / centre
    iterate = jnp.zeros_like(rhs_cols)
    remain = rhs_cols
    for sweep_index in range(sweeps):
        iterate = iterate + direction
        if sweep_index + 1 < sweeps:
            remain = remain - apply_fn(direction)
            factor_next = 1.0 / (2.0 * sig_ratio - factor)
            direction = factor_next * factor * direction + 2.0 * factor_next / half_width * remain
            factor = factor_next
    return iterate


def scaled(values, column_sum, column_sq, count):
    column_mean = column_sum / count
    column_var = column_sq / count - column_mean * column_mean
    inverse = 1.0 / jnp.sqrt(column_var + 1e-05)
    return ((values - column_mean) * inverse).astype(jnp.bfloat16)


def shards(dosages, new_dosages, traits, shrink):
    local_rows = dosages.shape[0]
    trait_count = traits.shape[0]
    count = float(local_rows * lax.axis_size("samp"))
    block_codes = dosages.astype(jnp.float32)
    new_codes = new_dosages.astype(jnp.float32)
    block_sum, block_sq, new_sum, new_sq = lax.psum(
        (
            jnp.sum(block_codes, axis=0),
            jnp.sum(block_codes * block_codes, axis=0),
            jnp.sum(new_codes, axis=0),
            jnp.sum(new_codes * new_codes, axis=0),
        ),
        "samp",
    )
    standard = scaled(block_codes, block_sum, block_sq, count)
    fresh = scaled(new_codes, new_sum, new_sq, count)
    trait_bf = traits.astype(jnp.bfloat16)
    gram = lax.dot_general(
        standard, standard, (((0,), (0,)), ((), ())), preferred_element_type=jnp.float32
    )
    cross = lax.dot_general(
        standard, trait_bf, (((0,), (1,)), ((), ())), preferred_element_type=jnp.float32
    )
    lam_cols = jnp.repeat(shrink, trait_count)
    gram_full, cross_full = lax.psum((gram, cross), "samp")
    bound = jnp.max(jnp.sum(jnp.abs(gram_full), axis=0)) / count

    def apply_full(direction):
        return (
            jnp.dot(gram_full, direction, precision=lax.Precision.HIGHEST) / count
            + lam_cols * direction
        )

    rhs_cols = jnp.tile(cross_full / count, (1, RIDGE))
    weights = chebyshev(
        rhs_cols, apply_full, lam_cols + bound / 2.0, bound / 2.0 + jnp.zeros_like(lam_cols), CHEB
    )
    weight_bf = weights.astype(jnp.bfloat16)
    pred = lax.dot_general(
        weight_bf, standard, (((0,), (1,)), ((), ())), preferred_element_type=jnp.float32
    )
    pred = pred.reshape(RIDGE, trait_count, local_rows)
    share = trait_count // lax.axis_size("blk")
    pred_part = lax.psum_scatter(pred, "blk", scatter_dimension=1, tiled=True)
    own_traits = lax.dynamic_slice_in_dim(traits, lax.axis_index("blk") * share, share, 0)
    residual = own_traits[None, :, :] - pred_part
    res_bf = lax.all_gather(residual.astype(jnp.bfloat16), "blk", axis=1, tiled=True)
    res_flat = res_bf.reshape(RIDGE * trait_count, local_rows)
    raw_part = jnp.dot(res_flat, fresh, preferred_element_type=jnp.float32)
    res_float = res_flat.astype(jnp.float32)
    raw, sum_sq = lax.psum((raw_part, jnp.sum(res_float * res_float, axis=1)), "samp")
    scores = raw / jnp.sqrt(count * (sum_sq / count + 1e-05))[:, None]
    return (residual, scores.reshape(RIDGE, trait_count, fresh.shape[1]))


def solution(mesh):
    placed = (P("samp", "blk"), P("samp", "blk"), P(None, "samp"), P())
    return jax.shard_map(
        shards,
        mesh=mesh,
        in_specs=placed,
        out_specs=(P(None, "blk", "samp"), P(None, None, "blk")),
        check_vma=False,
    )
```

profile of v0, /device:TPU:8, one launch (start us, length us, event | category | flops | bytes accessed | tf_op | source)
XLA Modules:
  0.0 635.6 jit_solution(12466145692508958539)
XLA Ops:
  7.2 0.0 all-reduce.12.cloned.1.call-start
  7.2 2.4 convert_reduce_fusion
  9.6 80.8 %all-reduce.2 = (f32[512]{0:T(512)S(1)}, f32[512]{0:T(512)S(1)}) all-reduce(f32[512]{0:T(512)S(1)} %get-tuple-element.3, f32[512]{0:T(512)S(1)} %get-tuple-element.2), channel_id=1, replica_groups=mesh['samp'=32,'blk'=16] {'samp'}, use_global_device_ids=true, to_apply=%region_3.0 | all-reduce | flops 1024 | bytes 8192 | tf_op jit(solution)/shard_map/psum | solution.py:39
  90.4 2.3 multiply_convert_fusion
  92.8 0.0 copy-start.2
  92.8 2.0 fusion.21
  94.8 0.0 copy-done.2
  94.8 0.0 copy-start.3
  94.8 1.0 fusion.16
  95.9 0.0 all-reduce.12.cloned.1.call-update
  95.9 0.0 all-reduce.10.cloned.1.call-start
  95.9 0.0 copy-done.3
  96.0 0.1 broadcast_in_dim.2
  96.0 0.1 reshape.58
  96.1 156.1 %all-reduce.12.cloned.1.call-done = (f32[512,64]{0,1:T(8,128)}, f32[512,512]{1,0:T(8,128)}) async-done(((f32[512,64]{0,1:T(8,128)}, f32[512,512]{1,0:T(8,128)}), (f32[512,64]{0,1:T(8,128)}, f32[512,512]{1,0:T(8,128)})) %all-reduce.12.cloned.1.call-update) | async-done | bytes 1179664 | tf_op jit(solution)/shard_map/psum | solution.py:58
  252.2 0.0 copy-start
  252.2 1.5 abs_reduce_fusion
  253.7 0.6 reduce_max.9
  255.0 0.9 broadcast_multiply_fusion
  255.9 0.1 bitcast_divide_fusion
  256.0 0.1 tile.4
  256.1 0.0 copy-done
  256.1 1.3 fusion.6
  257.4 1.6 fusion.7
  259.1 2.0 fusion.22
  261.1 0.0 copy-start.1
  261.1 0.0 all-reduce.10.cloned.1.call-update
  261.1 0.0 all-reduce.8.cloned.1.call-start
  261.2 1.3 dynamic-slice
  263.1 0.0 copy-done.1
  263.1 0.2 convert_reduce_fusion.1
  263.4 113.1 %all-reduce.10.cloned.1.call-done = f32[5,64,1536]{2,1,0:T(8,128)} async-done(((f32[5,64,1536]{2,1,0:T(8,128)}), f32[5,64,1536]{2,1,0:T(8,128)}) %all-reduce.10.cloned.1.call-update) | async-done | bytes 1966096
  376.5 1.6 fusion.20
  378.1 21.2 %all_gather.3 = bf16[5,64,1536]{2,0,1:T(8,128)(2,1)S(1)} all-gather(bf16[5,4,1536]{2,0,1:T(8,128)(2,1)S(1)} %copy.11), channel_id=1, replica_groups=mesh['samp'=32,'blk'=16] {'blk'}, dimensions={1}, use_global_device_ids=true | all-gather | bytes 1044480 | tf_op jit(solution)/shard_map/all_gather | solution.py:80
  399.4 0.5 multiply_reduce_fusion
  399.9 0.3 copy.12
  400.2 0.1 copy.13
  400.3 0.1 reduce_sum.62
  400.4 75.6 %all-reduce.1 = (f32[128]{0:T(128)S(1)}, f32[128]{0:T(128)S(1)}, f32[320]{0:T(512)S(1)}) all-reduce(f32[128]{0:T(128)S(1)} %get-tuple-element.5, f32[128]{0:T(128)S(1)} %get-tuple-element.4, f32[320]{0:T(512)S(1)} %reduce_sum.62), channel_id=1, replica_groups=mesh['samp'=32,'blk'=16] {'samp'}, use_global_device_ids=true, to_apply=%region_12.0 | all-reduce | flops 576 | bytes 4608 | tf_op jit(solution)/shard_map/psum | solution.py:39
  476.0 1.1 fusion.11
  477.1 0.0 all-reduce.8.cloned.1.call-update
  477.1 150.2 %all-reduce.8.cloned.1.call-done = f32[320,128]{1,0:T(8,128)} async-done(((f32[320,128]{1,0:T(8,128)}), f32[320,128]{1,0:T(8,128)}) %all-reduce.8.cloned.1.call-update) | async-done | bytes 163856 | tf_op jit(solution)/shard_map/psum | solution.py:84
  627.4 1.7 broadcast_divide_fusion
  (7 shorter events, 0.1 us)
Async XLA Ops:
  7.2 245.0 %all-reduce.12.cloned.1.call-start = ((), (), s32[]{:S(2)}) async-start(), calls=%async_computation.2 | async-start | bytes 2359296 | tf_op jit(solution)/shard_map/psum | solution.py:58
  92.8 2.1 copy-start.2
  94.8 1.1 copy-start.3
  95.9 280.6 %all-reduce.10.cloned.1.call-start = ((), (), s32[]{:S(2)}) async-start(), calls=%async_computation.1 | async-start | bytes 3932160
  252.2 3.9 copy-start
  261.1 2.1 copy-start.1
  261.1 366.3 %all-reduce.8.cloned.1.call-start = ((), (), s32[]{:S(2)}) async-start(), calls=%async_computation | async-start | bytes 327680 | tf_op jit(solution)/shard_map/psum | solution.py:84
Sparse Core Ops, SparseCore 0:
  96.0 156.1 all-reduce.11
  261.2 115.2 all-reduce.9
  477.2 150.0 all-reduce.7
where the time goes:
time: 636 us
  waiting for transfers between devices  419 us (66%)
  blocking collectives  178 us (28%)
  between operations  15.2 us (2%)
  other arithmetic  11.9 us (2%)
  matrix products  9.16 us (1%)
    psum x2, blocking collectives, shards(): lax.psum((jnp.sum(block_codes, axis=0), jnp.sum(block_codes * block_codes...  156 us
    psum x1, waiting for transfers between devices, shards(): gram_full, cross_full = lax.psum((gram, cross), 'samp')  156 us
    psum x1, waiting for transfers between devices, shards(): lax.psum((raw_part, jnp.sum(res_float * res_float, axis=1)), 'samp')  150 us
    unnamed x4, waiting for transfers between devices  113 us
    all_gather x1, blocking collectives, shards(): lax.all_gather(residual.astype(jnp.bfloat16), 'blk', axis=1, tiled=True)  21.2 us
  transfers between devices with their start and end apart: 3, of which 3 were waited for; matrix products, arithmetic and copies ran while one was open for 0% of the time, Pallas kernels for 0%

commit v1 on v0

--- a/solution.py
+++ b/solution.py
@@ -77,7 +77,12 @@
     pred_part = lax.psum_scatter(pred, "blk", scatter_dimension=1, tiled=True)
     own_traits = lax.dynamic_slice_in_dim(traits, lax.axis_index("blk") * share, share, 0)
     residual = own_traits[None, :, :] - pred_part
-    res_bf = lax.all_gather(residual.astype(jnp.bfloat16), "blk", axis=1, tiled=True)
+    res_bf = jnp.concatenate(
+        lax.all_to_all(
+            jnp.stack([residual.astype(jnp.bfloat16)] * lax.axis_size("blk")), "blk", 0, 0
+        ),
+        axis=1,
+    )
     res_flat = res_bf.reshape(RIDGE * trait_count, local_rows)
     raw_part = jnp.dot(res_flat, fresh, preferred_element_type=jnp.float32)
     res_float = res_flat.astype(jnp.float32)

time: 636 us -> 647 us (1.017)
  waiting for transfers between devices: 419 us -> 441 us
  blocking collectives: 178 us -> 157 us
  starting transfers between devices: 0.12 us -> 8.66 us
    all_to_all x0 -> x1, waiting for transfers between devices: none -> 22.9 us  [shards(): lax.all_to_all(jnp.stack([residual.astype(jnp.bfloat16)] * lax.axis_size(...]
    all_gather x1 -> x0, blocking collectives: 21.2 us -> none  [shards(): lax.all_gather(residual.astype(jnp.bfloat16), 'blk', axis=1, tiled=True)]
    all_to_all x0 -> x1, starting transfers between devices: none -> 8.55 us  [shards(): lax.all_to_all(jnp.stack([residual.astype(jnp.bfloat16)] * lax.axis_size(...]
  transfers between devices with their start and end apart: 3 -> 4, of which waited for: 3 -> 4; matrix products, arithmetic and copies ran while one was open for 0% -> 0% of each run, Pallas kernels for 0% -> 0%
where the time goes in v1:
time: 647 us; the launch traced here: 646 us
  waiting for transfers between devices  441 us (68%)
  blocking collectives  157 us (24%)
  between operations  15.2 us (2%)
  other arithmetic  12 us (2%)
  matrix products  9.16 us (1%)
  starting transfers between devices  8.66 us (1%)
    psum x2, blocking collectives, shards(): lax.psum((jnp.sum(block_codes, axis=0), jnp.sum(block_codes * block_codes...  157 us
    psum x1, waiting for transfers between devices, shards(): gram_full, cross_full = lax.psum((gram, cross), 'samp')  156 us
    psum x1, waiting for transfers between devices, shards(): lax.psum((raw_part, jnp.sum(res_float * res_float, axis=1)), 'samp')  149 us
    unnamed x4, waiting for transfers between devices  113 us
    all_to_all x1, waiting for transfers between devices, shards(): lax.all_to_all(jnp.stack([residual.astype(jnp.bfloat16)] * lax.axis_size(...  22.9 us
  transfers between devices with their start and end apart: 4, of which 4 were waited for; matrix products, arithmetic and copies ran while one was open for 0% of the time, Pallas kernels for 0%

profile of v1, /device:TPU:8, one launch (start us, length us, event | category | flops | bytes accessed | tf_op | source)
XLA Modules:
  0.0 646.1 jit_solution(5539306916869710371)
XLA Ops:
  7.2 0.0 all-reduce.12.cloned.1.call-start
  7.2 2.4 convert_reduce_fusion
  9.6 80.8 %all-reduce.2 = (f32[512]{0:T(512)S(1)}, f32[512]{0:T(512)S(1)}) all-reduce(f32[512]{0:T(512)S(1)} %get-tuple-element.3, f32[512]{0:T(512)S(1)} %get-tuple-element.2), channel_id=1, replica_groups=mesh['samp'=32,'blk'=16] {'samp'}, use_global_device_ids=true, to_apply=%region_3.0 | all-reduce | flops 1024 | bytes 8192 | tf_op jit(solution)/shard_map/psum | solution.py:39
  90.4 2.3 multiply_convert_fusion
  92.8 0.0 copy-start.2
  92.8 2.0 fusion.21
  94.8 0.0 copy-done.2
  94.8 0.0 copy-start.3
  94.8 1.0 fusion.16
  95.9 0.0 all-reduce.12.cloned.1.call-update
  95.9 0.0 all-reduce.10.cloned.1.call-start
  95.9 0.0 copy-done.3
  96.0 0.1 broadcast_in_dim.2
  96.0 0.1 reshape.60
  96.1 156.1 %all-reduce.12.cloned.1.call-done = (f32[512,64]{0,1:T(8,128)}, f32[512,512]{1,0:T(8,128)}) async-done(((f32[512,64]{0,1:T(8,128)}, f32[512,512]{1,0:T(8,128)}), (f32[512,64]{0,1:T(8,128)}, f32[512,512]{1,0:T(8,128)})) %all-reduce.12.cloned.1.call-update) | async-done | bytes 1179664 | tf_op jit(solution)/shard_map/psum | solution.py:58
  252.2 0.0 copy-start
  252.2 1.5 abs_reduce_fusion
  253.7 0.6 reduce_max.9
  255.0 0.9 broadcast_multiply_fusion
  255.9 0.1 bitcast_divide_fusion
  256.0 0.1 tile.4
  256.1 0.0 copy-done
  256.1 1.3 fusion.6
  257.4 1.6 fusion.7
  259.1 2.0 fusion.22
  261.1 0.0 all-reduce.10.cloned.1.call-update
  261.1 0.0 copy-start.1
  261.1 1.3 dynamic-slice
  263.1 113.3 %all-reduce.10.cloned.1.call-done = f32[5,64,1536]{2,1,0:T(8,128)} async-done(((f32[5,64,1536]{2,1,0:T(8,128)}), f32[5,64,1536]{2,1,0:T(8,128)}) %all-reduce.10.cloned.1.call-update) | async-done | bytes 1966096
  376.5 1.6 fusion.20
  378.1 1.2 stack.2
  379.3 8.5 %all-to-all-start = ((bf16[16,5,4,1536]{3,2,1,0:T(4,128)(2,1)}), bf16[16,5,4,1536]{3,2,1,0:T(4,128)(2,1)S(1)}, u32[]{:S(2)}, u32[]{:S(2)}) async-start(bf16[16,5,4,1536]{3,2,1,0:T(4,128)(2,1)} %stack.2), calls=%async_computation | async-start | bytes 1966080 | tf_op jit(solution)/shard_map/all_to_all | solution.py:81
  387.9 0.0 all-reduce.8.cloned.1.call-start
  387.9 0.0 copy-done.1
  387.9 0.2 convert_reduce_fusion.1
  388.1 22.9 %all-to-all-done = bf16[16,5,4,1536]{3,2,1,0:T(4,128)(2,1)S(1)} async-done(((bf16[16,5,4,1536]{3,2,1,0:T(4,128)(2,1)}), bf16[16,5,4,1536]{3,2,1,0:T(4,128)(2,1)S(1)}, u32[]{:S(2)}, u32[]{:S(2)}) %all-to-all-start) | async-done | bytes 983072 | tf_op jit(solution)/shard_map/all_to_all | solution.py:81
  411.1 0.6 multiply_reduce_fusion.1
  411.7 0.1 reduce_sum.62
  411.8 0.3 copy.7
  412.1 0.2 reshape_reshape.3
  412.4 75.7 %all-reduce.1 = (f32[128]{0:T(128)S(1)}, f32[128]{0:T(128)S(1)}, f32[320]{0:T(512)S(1)}) all-reduce(f32[128]{0:T(128)S(1)} %get-tuple-element.5, f32[128]{0:T(128)S(1)} %get-tuple-element.4, f32[320]{0:T(512)S(1)} %reduce_sum.62), channel_id=1, replica_groups=mesh['samp'=32,'blk'=16] {'samp'}, use_global_device_ids=true, to_apply=%region_12.0 | all-reduce | flops 576 | bytes 4608 | tf_op jit(solution)/shard_map/psum | solution.py:39
  488.1 1.1 fusion.11
  489.2 0.0 all-reduce.8.cloned.1.call-update
  489.2 148.7 %all-reduce.8.cloned.1.call-done = f32[320,128]{1,0:T(8,128)} async-done(((f32[320,128]{1,0:T(8,128)}), f32[320,128]{1,0:T(8,128)}) %all-reduce.8.cloned.1.call-update) | async-done | bytes 163856 | tf_op jit(solution)/shard_map/psum | solution.py:89
  637.9 1.7 broadcast_divide_fusion
  (7 shorter events, 0.1 us)
Async XLA Ops:
  7.2 245.0 %all-reduce.12.cloned.1.call-start = ((), (), s32[]{:S(2)}) async-start(), calls=%async_computation.3 | async-start | bytes 2359296 | tf_op jit(solution)/shard_map/psum | solution.py:58
  92.8 2.1 copy-start.2
  94.8 1.1 copy-start.3
  95.9 280.6 %all-reduce.10.cloned.1.call-start = ((), (), s32[]{:S(2)}) async-start(), calls=%async_computation.2 | async-start | bytes 3932160
  252.2 3.9 copy-start
  261.1 126.8 %copy-start.1 = (s32[1536,128]{1,0:T(8,128)S(1)}, s32[1536,128]{1,0:T(8,128)}, u32[]{:S(2)}) copy-start(s32[1536,128]{1,0:T(8,128)} %param.5) | copy-start | bytes 2359300
  379.3 31.8 %all-to-all-start = ((bf16[16,5,4,1536]{3,2,1,0:T(4,128)(2,1)}), bf16[16,5,4,1536]{3,2,1,0:T(4,128)(2,1)S(1)}, u32[]{:S(2)}, u32[]{:S(2)}) async-start(bf16[16,5,4,1536]{3,2,1,0:T(4,128)(2,1)} %stack.2), calls=%async_computation | async-start | bytes 1966080 | tf_op jit(solution)/shard_map/all_to_all | solution.py:81
  387.9 250.1 %all-reduce.8.cloned.1.call-start = ((), (), s32[]{:S(2)}) async-start(), calls=%async_computation.1 | async-start | bytes 327680 | tf_op jit(solution)/shard_map/psum | solution.py:89
Sparse Core Ops, SparseCore 0:
  96.0 156.1 all-reduce.11
  261.2 115.2 all-reduce.9
  489.3 148.5 all-reduce.7
